TPU v7x, 128 devices: a whole 4x4x4 slice. The times are simulated.
128 devices in a mesh: seq: 16 (over z_lo, y, core), head: 8 (over z_hi, x).
Axes of the slice: x: 4, y: 4, z: 4 (z_hi: 2, z_lo: 2; z = z_hi * 2 + z_lo), core: 2. Of those that a mesh axis runs over, the one named last changes fastest.
Arguments:
- queries: bfloat16 [8192, 4096], P('seq', 'head'), may hold values from -6 to 6
- new_keys: bfloat16 [8192, 4096], P('seq', 'head'), may hold values from -6 to 6
- new_values: bfloat16 [8192, 4096], P('seq', 'head'), may hold values from -6 to 6
- pool_keys: bfloat16 [16384, 4096], P('seq', 'head'), may hold values from -6 to 6
- pool_values: bfloat16 [16384, 4096], P('seq', 'head'), may hold values from -6 to 6
- cache_len: int32 [4], replicated, may hold values from 128 to 4096, as said below
- cached_table: int32 [4, 32], replicated, may hold values from -1 to 127, as said below
- free_blocks: int32 [4, 16], replicated, may hold values from 0 to 127, as said below
- residual_in: bfloat16 [8192, 7168], P('seq', 'head'), may hold values from -26 to 26
- out_weight: bfloat16 [4096, 7168], P('head'), may hold values from -2.390625 to 2.390625
- out_bias: float32 [7168], P('head'), may hold values from -3 to 3
- ln_gain: float32 [7168], P('head'), may hold values from 0.1 to 1.9
- ln_bias: float32 [7168], P('head'), may hold values from -3 to 3
Outputs:
- hidden: bfloat16 [8192, 7168], P('seq', 'head')
- normed: bfloat16 [8192, 7168], P('seq', 'head')
- keys_out: bfloat16 [16384, 4096], P('seq', 'head')
- values_out: bfloat16 [16384, 4096], P('seq', 'head')
Inputs may be any that keep to these rules, and one draw needn't show every extreme that they name: `cache_len`: a multiple of 128; exactly one prompt has 4096 cached positions. `cached_table`: entry [p, j] names the pool block that holds cached positions j * 128 to j * 128 + 127 of prompt p when j < cache_len[p] / 128, and is -1 otherwise; the named blocks are all different and lie anywhere in the pool. `free_blocks`: all different and never named by cached_table; block free_blocks[p, j] lies in the pool rows held by the same index of seq as token row p * 2048 + j * 128, that is free_blocks[p, j] * 128 // 1024 == (p * 2048 + j * 128) // 512.
All inputs are finite; a program needn't handle non-finite values.
Results may differ from a plain program's by a relative error of at most 0.022.
Values may be sent and summed in bfloat16 or wider, within the bound.
No kernel may reach another device: no remote copies, remote signals or barrier semaphores. Data moves between devices by JAX's collectives and lax.ppermute only.
A program may use at most 384 MiB of HBM per device.

v0:
```python
import jax
import jax.numpy as jnp
from jax import lax
from jax.sharding import PartitionSpec as P

D = 7168
HD = 128
NEW_LEN = 2048
BLOCK = 128
NEGATIVE = -1e30


def key_facts(block_count, cached_table, free_blocks, cache_len):
    block_ids = jnp.arange(block_count, dtype=jnp.int32)
    prompt_count, cached_count = cached_table.shape
    fresh_count = free_blocks.shape[1]
    prompt_ids = jnp.arange(prompt_count, dtype=jnp.int32)
    in_cache = cached_table[None, :, :] == block_ids[:, None, None]
    in_fresh = free_blocks[None, :, :] == block_ids[:, None, None]
    owner = jnp.sum(jnp.where(in_cache, prompt_ids[None, :, None] + 1, 0), axis=(1, 2))
    owner = owner + jnp.sum(jnp.where(in_fresh, prompt_ids[None, :, None] + 1, 0), axis=(1, 2)) - 1
    cached_slot = jnp.arange(cached_count, dtype=jnp.int32)
    fresh_slot = (cache_len // BLOCK)[:, None] + jnp.arange(fresh_count, dtype=jnp.int32)[None, :]
    logical = jnp.sum(jnp.where(in_cache, cached_slot[None, None, :], 0), axis=(1, 2))
    logical = logical + jnp.sum(jnp.where(in_fresh, fresh_slot[None, :, :], 0), axis=(1, 2))
    key_owner = jnp.repeat(owner, BLOCK)
    key_place = (logical[:, None] * BLOCK + jnp.arange(BLOCK, dtype=jnp.int32)[None, :]).reshape(-1)
    return (key_owner, key_place)


def query_facts(first_row, row_count, cache_len):
    rows = first_row + jnp.arange(row_count, dtype=jnp.int32)
    owner = rows // NEW_LEN
    place = rows % NEW_LEN
    prompt_ids = jnp.arange(cache_len.shape[0], dtype=jnp.int32)
    limit = (
        jnp.sum(jnp.where(owner[:, None] == prompt_ids[None, :], cache_len[None, :], 0), axis=1)
        + place
    )
    return (owner, limit)


def attend(query_rows, query_owner, query_limit, keys, values, key_owner, key_place):
    row_count = query_rows.shape[0]
    heads_here = query_rows.shape[1] // HD
    key_count = keys.shape[0]
    query_split = query_rows.reshape(row_count, heads_here, HD)
    key_split = keys.reshape(key_count, heads_here, HD)
    value_split = values.reshape(key_count, heads_here, HD)
    visible = (key_owner[None, :] == query_owner[:, None]) & (
        key_place[None, :] <= query_limit[:, None]
    )
    scores = jnp.einsum(
        "rhd,khd->hrk", query_split, key_split, preferred_element_type=jnp.float32
    ) * HD ** (-0.5)
    scores = jnp.where(visible[None, :, :], scores, NEGATIVE)
    peak = jnp.max(scores, axis=2)
    weights = jnp.where(visible[None, :, :], jnp.exp(scores - peak[:, :, None]), 0.0)
    total = jnp.sum(weights, axis=2)
    mixed = jnp.einsum(
        "hrk,khd->rhd",
        weights.astype(jnp.bfloat16),
        value_split,
        preferred_element_type=jnp.float32,
    )
    return (peak.T, total.T, mixed.reshape(row_count, heads_here * HD))


def combine(first, second):
    peak = jnp.maximum(first[0], second[0])
    scale_first = jnp.exp(first[0] - peak)
    scale_second = jnp.exp(second[0] - peak)
    total = second[1] * scale_second
    row_count, heads_here = peak.shape
    mixed = first[2].reshape(row_count, heads_here, HD) * scale_first[:, :, None]
    mixed = second[2].reshape(row_count, heads_here, HD) * scale_second[:, :, None]
    return (peak, total, mixed.reshape(row_count, heads_here * HD))


def shards(
    queries,
    new_keys,
    new_values,
    pool_keys,
    pool_values,
    cache_len,
    cached_table,
    free_blocks,
    residual_in,
    out_weight,
    out_bias,
    ln_gain,
    ln_bias,
):
    token_rows, width = queries.shape
    heads_here = width // HD
    pool_rows = pool_keys.shape[0]
    per_device = pool_rows // BLOCK
    fresh_device = token_rows // BLOCK
    position = lax.axis_index("seq")
    first_row = position * token_rows
    prompt_here = first_row // NEW_LEN
    first_slot = first_row % NEW_LEN // BLOCK
    targets = (
        lax.dynamic_slice(free_blocks, (prompt_here, first_slot), (1, fresh_device))[0]
        - position * per_device
    )
    keys_out = (
        pool_keys.reshape(per_device, BLOCK, width)
        .at[targets]
        .set(new_keys.reshape(fresh_device, BLOCK, width))
        .reshape(pool_rows, width)
    )
    values_out = (
        pool_values.reshape(per_device, BLOCK, width)
        .at[targets]
        .set(new_values.reshape(fresh_device, BLOCK, width))
        .reshape(pool_rows, width)
    )
    own_owner, own_limit = query_facts(first_row, token_rows, cache_len)
    start_state = (
        jnp.full((token_rows, heads_here), NEGATIVE, jnp.float32),
        jnp.zeros((token_rows, heads_here), jnp.float32),
        jnp.zeros((token_rows, width), jnp.float32),
    )
    piece_keys = lax.all_gather(keys_out, "seq", axis=0, tiled=True)
    piece_values = lax.all_gather(values_out, "seq", axis=0, tiled=True)
    key_owner, key_place = key_facts(
        piece_keys.shape[0] // BLOCK, cached_table, free_blocks, cache_len
    )
    peak, total, mixed = combine(
        start_state,
        attend(queries, own_owner, own_limit, piece_keys, piece_values, key_owner, key_place),
    )
    attn = (
        (mixed.reshape(token_rows, heads_here, HD) / total[:, :, None])
        .reshape(token_rows, width)
        .astype(jnp.bfloat16)
    )
    projected = jnp.dot(attn, out_weight, preferred_element_type=jnp.float32)
    summed = lax.psum_scatter(
        projected.astype(jnp.bfloat16), "head", scatter_dimension=1, tiled=True
    ).astype(jnp.float32)
    stream = residual_in.astype(jnp.float32) + summed + out_bias[None, :]
    mean = lax.psum(jnp.sum(stream, axis=1), "head") / D
    centred = stream - mean[:, None]
    variance = lax.psum(jnp.sum(centred * centred, axis=1), "head") / D
    normed = (
        centred * lax.rsqrt(variance[:, None] + 1e-05) * ln_gain[None, :] + ln_bias[None, :]
    ).astype(jnp.bfloat16)
    return (stream.astype(jnp.bfloat16), normed, keys_out, values_out)


def solution(mesh):
    in_specs = (
        P("seq", "head"),
        P("seq", "head"),
        P("seq", "head"),
        P("seq", "head"),
        P("seq", "head"),
        P(),
        P(),
        P(),
        P("seq", "head"),
        P("head", None),
        P("head"),
        P("head"),
        P("head"),
    )
    out_specs = (P("seq", "head"), P("seq", "head"), P("seq", "head"), P("seq", "head"))
    return jax.shard_map(shards, mesh=mesh, in_specs=in_specs, out_specs=out_specs, check_vma=False)
```

profile of v0, /device:TPU:0, one launch (start us, length us, event | category | flops | bytes accessed | tf_op | source)
XLA Modules:
  0.0 465.4 jit_solution(8003422405766926117)
XLA Ops:
  7.2 0.0 copy-start
  7.2 0.0 all-gather.5.cloned.1.call-start
  7.2 1.3 copy.59
  8.5 1.2 copy.60
  9.7 0.8 fusion.22
  10.5 1.7 scatter_fusion.1
  12.2 0.0 copy-start.4
  12.2 1.3 copy.38
  13.5 0.0 all-gather.5.cloned.1.call-update
  13.5 0.0 all-gather.3.cloned.1.call-start
  13.6 1.7 scatter_fusion
  15.3 0.0 copy-start.3
  15.3 1.0 copy-done.3
  16.3 0.0 all-gather.3.cloned.1.call-update
  16.3 0.0 reduce-scatter.4.cloned.1.call-start
  16.4 0.7 select_reduce_fusion.4
  17.1 0.8 select_reduce_fusion.1
  17.9 0.7 and_select_fusion
  18.6 0.1 iota_add_fusion
  18.6 0.8 select_reduce_fusion.3
  19.4 0.1 add_bitcast_fusion
  19.5 0.1 broadcast_bitcast_fusion
  19.6 13.3 %compare_and_fusion = pred[512,16384]{0,1:T(8,128)(4,1)} fusion(s32[512]{0:T(512)S(1)} %fusion.18, s32[512]{0:T(512)S(1)} %add_select_fusion.1, s32[16384]{0:T(1024)S(1)} %add_bitcast_fusion, s32[16384]{0:T(1024)S(1)} %broadcast_bitcast_fusion), kind=kLoop, calls=%fused_computation.9 | loop fusion | flops 25165824 | bytes 8523776 | tf_op jit(solution)/shard_map/and | solution.py:50
  32.9 74.9 %all-gather.5.cloned.1.call-done = bf16[16384,512]{0,1:T(8,128)(2,1)} async-done(((bf16[1024,512]{0,1:T(8,128)(2,1)}), bf16[16384,512]{0,1:T(8,128)(2,1)}) %all-gather.5.cloned.1.call-update) | async-done | bytes 16777232 | tf_op jit(solution)/shard_map/all_gather | solution.py:126
  107.8 0.0 copy-done
  107.8 59.0 %fusion = (f32[4,512]{1,0:T(4,128)S(1)}, f32[4,16384,512]{2,1,0:T(8,128)}) fusion(pred[512,16384]{0,1:T(8,128)(4,1)} %compare_and_fusion, bf16[16384,4,128]{0,2,1:T(8,128)(2,1)} %bitcast.79, bf16[512,512]{1,0:T(8,128)(2,1)S(1)} %copy-done), kind=kOutput, calls=%fused_computation.4 | convolution fusion | flops 8690595840 | bytes 159916032 | tf_op jit(solution)/shard_map/rhd,khd->hrk/dot_general | solution.py:53
  166.8 0.0 copy-done.4
  166.8 45.4 %fusion.1 = f32[4,512]{1,0:T(4,128)S(1)} fusion(f32[4,16384,512]{2,1,0:T(8,128)} %get-tuple-element.17, f32[4,512]{1,0:T(4,128)S(1)} %get-tuple-element.16, pred[512,16384]{0,1:T(8,128)(4,1)} %compare_and_fusion), kind=kLoop, calls=%fused_computation.5 | loop fusion | flops 167770112 | bytes 142622720 | tf_op jit(solution)/shard_map/reduce_sum | solution.py:59
  212.2 0.0 all-gather.3.cloned.1.call-done
  212.2 21.3 %copy.37 = bf16[16384,512]{0,1:T(8,128)(2,1)} copy(bf16[16384,512]{1,0:T(8,128)(2,1)} %all-gather.3.cloned.1.call-done) | data formatting | bytes 33554432 | tf_op jit(solution)/shard_map/all_gather | solution.py:127
  233.5 52.8 %divide_convert_fusion = bf16[512,4,128]{0,2,1:T(8,128)(2,1)S(1)} fusion(f32[512,4]{0,1:T(4,128)S(1)} %get-tuple-element.14, f32[512,4]{0,1:T(4,128)S(1)} %get-tuple-element.15, bf16[16384,4,128]{0,2,1:T(8,128)(2,1)} %bitcast.68, f32[4,16384,512]{2,1,0:T(8,128)} %get-tuple-element.17, f32[4,512]{1,0:T(4,128)S(1)} %get-tuple-element.16, ...), kind=kOutput, calls=%fused_computation.18 | convolution fusion | flops 8758493184 | bytes 159932416 | tf_op jit(solution)/shard_map/hrk,khd->rhd/dot_general | solution.py:60
  286.3 0.0 copy-start.2
  286.3 0.0 copy-start.5
  286.3 0.0 copy-start.1
  286.3 9.5 %convolution_convert_fusion = bf16[512,7168]{1,0:T(8,128)(2,1)} fusion(bf16[512,512]{0,1:T(8,128)(2,1)S(1)} %bitcast.78, bf16[512,7168]{1,0:T(8,128)(2,1)} %param.22), kind=kOutput, calls=%fused_computation.10 | convolution fusion | flops 3761766400 | bytes 15204352 | tf_op jit(solution)/shard_map/dot_general | solution.py:140
  295.9 0.0 copy-start.6
  295.9 0.0 copy-start.7
  295.9 10.4 %copy.44 = bf16[512,7168]{0,1:T(8,128)(2,1)} copy(bf16[512,7168]{1,0:T(8,128)(2,1)} %convolution_convert_fusion) | data formatting | bytes 14680064
  306.3 0.0 reduce-scatter.4.cloned.1.call-update
  306.3 108.4 %reduce-scatter.4.cloned.1.call-done = bf16[896,512]{1,0:T(8,128)(2,1)} async-done(((bf16[7168,512]{1,0:T(8,128)(2,1)}), bf16[896,512]{1,0:T(8,128)(2,1)}) %reduce-scatter.4.cloned.1.call-update) | async-done | bytes 917520
  414.7 1.5 copy.45
  416.3 0.0 copy-done.2
  416.3 0.0 copy-done.5
  416.3 0.4 fusion.12
  416.7 20.3 %psum.14 = f32[512]{0:T(512)S(1)} all-reduce(f32[512]{0:T(512)S(1)} %fusion.12), channel_id=1, replica_groups=mesh['seq'=16,'head'=8] {'head'}, use_global_device_ids=true, to_apply=%region_11.12 | all-reduce | flops 512 | bytes 4096 | tf_op jit(solution)/shard_map/psum | solution.py:145
  437.0 0.5 multiply_reduce_fusion
  437.5 19.6 %psum.15 = f32[512]{0:T(512)S(1)} all-reduce(f32[512]{0:T(512)S(1)} %multiply_reduce_fusion), channel_id=1, replica_groups=mesh['seq'=16,'head'=8] {'head'}, use_global_device_ids=true, to_apply=%region_13.14 | all-reduce | flops 512 | bytes 4096 | tf_op jit(solution)/shard_map/psum | solution.py:147
  457.1 0.0 copy-done.6
  457.1 0.0 copy-done.7
  457.1 1.8 add_convert_fusion
  458.9 0.0 copy-done.1
  (7 shorter events, 0.1 us)
Async XLA Ops:
  7.2 100.6 %copy-start = (bf16[512,512]{1,0:T(8,128)(2,1)S(1)}, bf16[512,512]{1,0:T(8,128)(2,1)}, u32[]{:S(2)}) copy-start(bf16[512,512]{1,0:T(8,128)(2,1)} %param.13) | copy-start | bytes 1572868
  7.2 100.6 %all-gather.5.cloned.1.call-start = ((), (), s32[]{:S(2)}) async-start(), calls=%async_computation.2 | async-start | bytes 17825792 | tf_op jit(solution)/shard_map/all_gather | solution.py:126
  12.2 154.6 %copy-start.4 = (bf16[8,128,512]{2,1,0:T(8,128)(2,1)}, bf16[8,128,512]{2,1,0:T(8,128)(2,1)S(1)}, u32[]{:S(2)}) copy-start(bf16[8,128,512]{2,1,0:T(8,128)(2,1)S(1)} %scatter_fusion.1) | copy-start | bytes 3145732
  13.5 198.6 %all-gather.3.cloned.1.call-start = ((), (), s32[]{:S(2)}) async-start(), calls=%async_computation.1 | async-start | bytes 17825792 | tf_op jit(solution)/shard_map/all_gather | solution.py:127
  15.3 1.0 copy-start.3
  16.3 398.4 %reduce-scatter.4.cloned.1.call-start = ((), (), s32[]{:S(2)}) async-start(), calls=%async_computation.3 | async-start | bytes 8257536
  286.3 130.0 %copy-start.2 = (bf16[512,896]{1,0:T(8,128)(2,1)S(1)}, bf16[512,896]{1,0:T(8,128)(2,1)}, u32[]{:S(2)}) copy-start(bf16[512,896]{1,0:T(8,128)(2,1)} %param.21) | copy-start | bytes 2752516
  286.3 130.0 %copy-start.5 = (f32[896]{0:T(1024)S(1)}, f32[896]{0:T(1024)}, u32[]{:S(2)}) copy-start(f32[896]{0:T(1024)} %param.23) | copy-start | bytes 10756
  286.3 172.6 %copy-start.1 = (bf16[512,512]{1,0:T(8,128)(2,1)S(1)}, bf16[512,512]{1,0:T(8,128)(2,1)}, u32[]{:S(2)}) copy-start(bf16[512,512]{1,0:T(8,128)(2,1)} %param.13) | copy-start | bytes 1572868
  295.9 161.2 %copy-start.6 = (f32[896]{0:T(1024)S(1)}, f32[896]{0:T(1024)}, u32[]{:S(2)}) copy-start(f32[896]{0:T(1024)} %param.25) | copy-start | bytes 10756
  295.9 161.2 %copy-start.7 = (f32[896]{0:T(1024)S(1)}, f32[896]{0:T(1024)}, u32[]{:S(2)}) copy-start(f32[896]{0:T(1024)} %param.24) | copy-start | bytes 10756
Sparse Core Ops, SparseCore 0:
  13.7 94.0 all-gather.4
  110.1 92.4 all-gather.2
  306.5 108.2 reduce-scatter.3
where the time goes:
time: 467 us; the launch traced here: 465 us
  waiting for transfers between devices  183 us (39%)
  matrix products  121 us (26%)
  other arithmetic  65.2 us (14%)
  local copies, waits for them, and re-layouts  41.5 us (9%)
  blocking collectives  39.9 us (9%)
  between operations  13.9 us (3%)
    unnamed x4, waiting for transfers between devices  108 us
    all_gather x1, waiting for transfers between devices, shards(): piece_keys = lax.all_gather(keys_out, 'seq', axis=0, tiled=True)  74.9 us
    dot_general x1, matrix products, attend(): jnp.einsum('rhd,khd->hrk', query_split, key_split, preferred_element_type...  59 us
    dot_general x1, matrix products, attend(): jnp.einsum('hrk,khd->rhd', weights.astype(jnp.bfloat16), value_split, pre...  52.8 us
    reduce_sum x1, other arithmetic, attend(): total = jnp.sum(weights, axis=2)  45.4 us
    all_gather x1, local copies, waits for them, and re-layouts, shards(): piece_values = lax.all_gather(values_out, 'seq', axis=0, tiled=True)  21.3 us
    psum x1, blocking collectives, shards(): mean = lax.psum(jnp.sum(stream, axis=1), 'head') / D  20.3 us
    psum x1, blocking collectives, shards(): variance = lax.psum(jnp.sum(centred * centred, axis=1), 'head') / D  19.6 us
  transfers between devices with their start and end apart: 3, of which 2 were waited for; matrix products, arithmetic and copies ran while one was open for 26% of the time, Pallas kernels for 0%

commit v1 on v0

--- a/solution.py
+++ b/solution.py
@@ -123,8 +123,11 @@
         jnp.zeros((token_rows, heads_here), jnp.float32),
         jnp.zeros((token_rows, width), jnp.float32),
     )
-    piece_keys = lax.all_gather(keys_out, "seq", axis=0, tiled=True)
-    piece_values = lax.all_gather(values_out, "seq", axis=0, tiled=True)
+    piece_keys, piece_values = jnp.split(
+        lax.all_gather(jnp.concatenate([keys_out, values_out], axis=1), "seq", axis=0, tiled=True),
+        [keys_out.shape[1]],
+        axis=1,
+    )
     key_owner, key_place = key_facts(
         piece_keys.shape[0] // BLOCK, cached_table, free_blocks, cache_len
     )

time: 467 us -> 548 us (1.17)
  waiting for transfers between devices: 183 us -> 268 us
    all_gather x2 -> x1, waiting for transfers between devices: 74.9 us -> 159 us  [shards(): lax.all_gather(jnp.concatenate([keys_out, values_out], axis=1), 'seq', ax...]
    split x0 -> x1, local copies, waits for them, and re-layouts: none -> 22.8 us  [shards(): jnp.split(lax.all_gather(jnp.concatenate([keys_out, values_out], axis=1),...]
    all_gather x1 -> x0, local copies, waits for them, and re-layouts: 21.3 us -> none  [shards(): piece_values = lax.all_gather(values_out, 'seq', axis=0, tiled=True)]
    unnamed x20 -> x26, local copies, waits for them, and re-layouts: 15.5 us -> 14.6 us
    unnamed x4 -> x3, waiting for transfers between devices: 108 us -> 109 us
  transfers between devices with their start and end apart: 3 -> 2, of which waited for: 2 -> 2; matrix products, arithmetic and copies ran while one was open for 26% -> 3% of each run, Pallas kernels for 0% -> 0%
where the time goes in v1:
time: 548 us
  waiting for transfers between devices  268 us (49%)
  matrix products  118 us (22%)
  other arithmetic  64 us (12%)
  local copies, waits for them, and re-layouts  43.5 us (8%)
  blocking collectives  39.9 us (7%)
  between operations  14.2 us (3%)
    all_gather x1, waiting for transfers between devices, shards(): lax.all_gather(jnp.concatenate([keys_out, values_out], axis=1), 'seq', ax...  159 us
    unnamed x3, waiting for transfers between devices  109 us
    dot_general x1, matrix products, attend(): jnp.einsum('rhd,khd->hrk', query_split, key_split, preferred_element_type...  55.8 us
    dot_general x1, matrix products, attend(): jnp.einsum('hrk,khd->rhd', weights.astype(jnp.bfloat16), value_split, pre...  52.8 us
    reduce_sum x1, other arithmetic, attend(): total = jnp.sum(weights, axis=2)  43.7 us
    split x1, local copies, waits for them, and re-layouts, shards(): jnp.split(lax.all_gather(jnp.concatenate([keys_out, values_out], axis=1),...  22.8 us
    psum x1, blocking collectives, shards(): mean = lax.psum(jnp.sum(stream, axis=1), 'head') / D  20.3 us
    psum x1, blocking collectives, shards(): variance = lax.psum(jnp.sum(centred * centred, axis=1), 'head') / D  19.6 us
  transfers between devices with their start and end apart: 2, of which 2 were waited for; matrix products, arithmetic and copies ran while one was open for 3% of the time, Pallas kernels for 0%

profile of v1, /device:TPU:0, one launch (start us, length us, event | category | flops | bytes accessed | tf_op | source)
XLA Modules:
  0.0 547.9 jit_solution(17023375459639259488)
XLA Ops:
  7.2 0.0 copy-start
  7.2 0.0 copy-start.10
  7.2 0.0 copy-start.9
  7.2 0.0 copy-start.8
  7.2 0.0 all-gather.2.cloned.1.call-start
  7.3 1.3 copy.61
  8.5 1.2 copy.62
  9.8 0.8 fusion.22
  10.5 1.7 scatter_fusion
  12.2 0.0 copy-start.4
  12.2 1.3 copy.39
  13.6 1.7 scatter_fusion.1
  15.3 0.0 copy-start.3
  15.3 1.3 copy.40
  16.6 3.0 pad_maximum_fusion
  19.6 0.0 all-gather.2.cloned.1.call-update
  19.7 0.0 reduce-scatter.4.cloned.1.call-start
  19.7 0.0 copy-done.10
  19.7 0.1 select_reduce_fusion.4
  19.8 0.0 copy-done.9
  19.8 0.1 select_reduce_fusion.1
  20.0 0.1 iota_add_fusion
  20.0 0.0 copy-done.8
  20.0 0.1 select_reduce_fusion.3
  20.2 0.1 add_bitcast_fusion
  20.2 0.1 broadcast_bitcast_fusion
  20.3 13.3 %compare_and_fusion = pred[512,16384]{0,1:T(8,128)(4,1)} fusion(s32[512]{0:T(512)S(1)} %fusion.18, s32[512]{0:T(512)S(1)} %add_select_fusion.1, s32[16384]{0:T(1024)S(1)} %add_bitcast_fusion, s32[16384]{0:T(1024)S(1)} %broadcast_bitcast_fusion), kind=kLoop, calls=%fused_computation.9 | loop fusion | flops 25165824 | bytes 8523776 | tf_op jit(solution)/shard_map/and | solution.py:50
  33.6 159.3 %all-gather.2.cloned.1.call-done = bf16[16384,1024]{0,1:T(8,128)(2,1)} async-done(((bf16[1024,1024]{0,1:T(8,128)(2,1)}), bf16[16384,1024]{0,1:T(8,128)(2,1)}) %all-gather.2.cloned.1.call-update) | async-done | bytes 33554448 | tf_op jit(solution)/shard_map/all_gather | solution.py:127
  192.9 22.8 %fusion.26 = (bf16[16384,512]{0,1:T(8,128)(2,1)}, bf16[16384,512]{0,1:T(8,128)(2,1)}) fusion(bf16[16384,1024]{0,1:T(8,128)(2,1)} %all-gather.2.cloned.1.call-done), kind=kLoop, calls=%fused_computation.62 | loop fusion | bytes 67108864 | tf_op jit(solution)/shard_map/split | solution.py:126
  215.7 0.0 copy-done.4
  215.8 0.0 copy-done.3
  215.8 0.0 copy-done
  215.8 55.8 %fusion = (f32[4,512]{1,0:T(4,128)S(1)}, f32[4,16384,512]{2,1,0:T(8,128)}) fusion(pred[512,16384]{0,1:T(8,128)(4,1)} %compare_and_fusion, bf16[16384,4,128]{0,2,1:T(8,128)(2,1)} %bitcast.69, bf16[512,512]{1,0:T(8,128)(2,1)S(1)} %copy-done), kind=kOutput, calls=%fused_computation.4 | convolution fusion | flops 8690595840 | bytes 159916032 | tf_op jit(solution)/shard_map/rhd,khd->hrk/dot_general | solution.py:53
  271.6 43.7 %fusion.1 = f32[4,512]{1,0:T(4,128)S(1)} fusion(f32[4,16384,512]{2,1,0:T(8,128)} %get-tuple-element.19, f32[4,512]{1,0:T(4,128)S(1)} %get-tuple-element.18, pred[512,16384]{0,1:T(8,128)(4,1)} %compare_and_fusion), kind=kLoop, calls=%fused_computation.5 | loop fusion | flops 167770112 | bytes 142622720 | tf_op jit(solution)/shard_map/reduce_sum | solution.py:59
  315.3 52.8 %divide_convert_fusion = bf16[512,4,128]{0,2,1:T(8,128)(2,1)S(1)} fusion(f32[512,4]{0,1:T(4,128)S(1)} %get-tuple-element.16, f32[512,4]{0,1:T(4,128)S(1)} %get-tuple-element.17, bf16[16384,4,128]{0,2,1:T(8,128)(2,1)} %bitcast.68, f32[4,16384,512]{2,1,0:T(8,128)} %get-tuple-element.19, f32[4,512]{1,0:T(4,128)S(1)} %get-tuple-element.18, ...), kind=kOutput, calls=%fused_computation.19 | convolution fusion | flops 8758493184 | bytes 159932416 | tf_op jit(solution)/shard_map/hrk,khd->rhd/dot_general | solution.py:60
  368.2 0.0 copy-start.1
  368.2 9.4 %convolution_convert_fusion = bf16[512,7168]{1,0:T(8,128)(2,1)} fusion(bf16[512,512]{0,1:T(8,128)(2,1)S(1)} %bitcast.79, bf16[512,7168]{1,0:T(8,128)(2,1)} %param.22), kind=kOutput, calls=%fused_computation.10 | convolution fusion | flops 3761766400 | bytes 15204352 | tf_op jit(solution)/shard_map/dot_general | solution.py:143
  377.6 0.0 copy-start.2
  377.6 0.0 copy-start.5
  377.6 0.0 copy-start.6
  377.6 0.0 copy-start.7
  377.6 10.5 %copy.46 = bf16[512,7168]{0,1:T(8,128)(2,1)} copy(bf16[512,7168]{1,0:T(8,128)(2,1)} %convolution_convert_fusion) | data formatting | bytes 14680064
  388.1 0.0 reduce-scatter.4.cloned.1.call-update
  388.1 108.7 %reduce-scatter.4.cloned.1.call-done = bf16[896,512]{1,0:T(8,128)(2,1)} async-done(((bf16[7168,512]{1,0:T(8,128)(2,1)}), bf16[896,512]{1,0:T(8,128)(2,1)}) %reduce-scatter.4.cloned.1.call-update) | async-done | bytes 917520
  496.9 1.5 copy.47
  498.4 0.0 copy-done.2
  498.4 0.0 copy-done.5
  498.4 0.4 fusion.12
  498.8 20.3 %psum.14 = f32[512]{0:T(512)S(1)} all-reduce(f32[512]{0:T(512)S(1)} %fusion.12), channel_id=1, replica_groups=mesh['seq'=16,'head'=8] {'head'}, use_global_device_ids=true, to_apply=%region_11.12 | all-reduce | flops 512 | bytes 4096 | tf_op jit(solution)/shard_map/psum | solution.py:148
  519.1 0.5 multiply_reduce_fusion
  519.7 19.6 %psum.15 = f32[512]{0:T(512)S(1)} all-reduce(f32[512]{0:T(512)S(1)} %multiply_reduce_fusion), channel_id=1, replica_groups=mesh['seq'=16,'head'=8] {'head'}, use_global_device_ids=true, to_apply=%region_13.14 | all-reduce | flops 512 | bytes 4096 | tf_op jit(solution)/shard_map/psum | solution.py:150
  539.2 0.0 copy-done.6
  539.2 0.0 copy-done.7
  539.2 1.8 add_convert_fusion
  541.0 0.0 copy-done.1
  (8 shorter events, 0.1 us)
Async XLA Ops:
  7.2 208.6 %copy-start = (bf16[512,512]{1,0:T(8,128)(2,1)S(1)}, bf16[512,512]{1,0:T(8,128)(2,1)}, u32[]{:S(2)}) copy-start(bf16[512,512]{1,0:T(8,128)(2,1)} %param.13) | copy-start | bytes 1572868
  7.2 12.6 %copy-start.10 = (s32[4]{0:T(128)S(1)}, s32[4]{0:T(128)}, u32[]{:S(2)}) copy-start(s32[4]{0:T(128)} %param.18) | copy-start | bytes 52
  7.2 12.6 %copy-start.9 = (s32[4,32]{1,0:T(4,128)S(1)}, s32[4,32]{1,0:T(4,128)}, u32[]{:S(2)}) copy-start(s32[4,32]{1,0:T(4,128)} %param.19) | copy-start | bytes 1540
  7.2 12.8 %copy-start.8 = (s32[4,16]{1,0:T(4,128)S(1)}, s32[4,16]{1,0:T(4,128)}, u32[]{:S(2)}) copy-start(s32[4,16]{1,0:T(4,128)} %param.20) | copy-start | bytes 772
  7.2 185.7 %all-gather.2.cloned.1.call-start = ((), (), s32[]{:S(2)}) async-start(), calls=%async_computation.1 | async-start | bytes 35651584 | tf_op jit(solution)/shard_map/all_gather | solution.py:127
  12.2 203.5 %copy-start.4 = (bf16[8,128,512]{2,1,0:T(8,128)(2,1)}, bf16[8,128,512]{2,1,0:T(8,128)(2,1)S(1)}, u32[]{:S(2)}) copy-start(bf16[8,128,512]{2,1,0:T(8,128)(2,1)S(1)} %scatter_fusion) | copy-start | bytes 3145732
  15.3 200.5 %copy-start.3 = (bf16[8,128,512]{2,1,0:T(8,128)(2,1)}, bf16[8,128,512]{2,1,0:T(8,128)(2,1)S(1)}, u32[]{:S(2)}) copy-start(bf16[8,128,512]{2,1,0:T(8,128)(2,1)S(1)} %scatter_fusion.1) | copy-start | bytes 3145732
  19.7 477.2 %reduce-scatter.4.cloned.1.call-start = ((), (), s32[]{:S(2)}) async-start(), calls=%async_computation.2 | async-start | bytes 8257536
  368.2 172.9 %copy-start.1 = (bf16[512,512]{1,0:T(8,128)(2,1)S(1)}, bf16[512,512]{1,0:T(8,128)(2,1)}, u32[]{:S(2)}) copy-start(bf16[512,512]{1,0:T(8,128)(2,1)} %param.13) | copy-start | bytes 1572868
  377.6 120.8 %copy-start.2 = (bf16[512,896]{1,0:T(8,128)(2,1)S(1)}, bf16[512,896]{1,0:T(8,128)(2,1)}, u32[]{:S(2)}) copy-start(bf16[512,896]{1,0:T(8,128)(2,1)} %param.21) | copy-start | bytes 2752516
  377.6 120.8 %copy-start.5 = (f32[896]{0:T(1024)S(1)}, f32[896]{0:T(1024)}, u32[]{:S(2)}) copy-start(f32[896]{0:T(1024)} %param.23) | copy-start | bytes 10756
  377.6 161.6 %copy-start.6 = (f32[896]{0:T(1024)S(1)}, f32[896]{0:T(1024)}, u32[]{:S(2)}) copy-start(f32[896]{0:T(1024)} %param.25) | copy-start | bytes 10756
  377.6 161.6 %copy-start.7 = (f32[896]{0:T(1024)S(1)}, f32[896]{0:T(1024)}, u32[]{:S(2)}) copy-start(f32[896]{0:T(1024)} %param.24) | copy-start | bytes 10756
Sparse Core Ops, SparseCore 0:
  19.8 173.1 all-gather.1
  388.3 108.5 reduce-scatter.3
